TPU v7x, 32 devices: a whole 2x2x4 slice. The times are simulated.
32 devices in a mesh: grp: 4 (over x, core), seq: 8 (over z, y).
Axes of the slice: x: 2, y: 2, z: 4, core: 2. Of those that a mesh axis runs over, the one named last changes fastest.
Arguments:
- signal: float32 [64, 2048, 768], P('grp', 'seq'), may hold values from -36 to 36
- entry_gain: float32 [768], replicated
- entry_shift: float32 [768], replicated, may hold values from -3 to 3
- dilated_kernel: float32 [3, 768, 384], replicated
- middle_gain: float32 [384], replicated
- middle_shift: float32 [384], replicated, may hold values from -3 to 3
- pointwise_kernel: float32 [384, 768], replicated
- pointwise_bias: float32 [768], replicated, may hold values from -3 to 3
- lengths: int32 [64], replicated, may hold values from 128 to 1024, as said below
- assignment: int32 [4, 16], P('grp'), may hold values from 0 to 15, as said below
- cotangent: float32 [65536, 768], P(('grp', 'seq')), may hold values from -6 to 6
Outputs:
- activations: float32 [65536, 768], P(('grp', 'seq'))
- signal_gradient: float32 [64, 2048, 768], P('grp', 'seq')
- entry_gain_gradient: float32 [768], replicated
- entry_shift_gradient: float32 [768], replicated
- dilated_kernel_gradient: float32 [3, 768, 384], replicated
- middle_gain_gradient: float32 [384], replicated
- middle_shift_gradient: float32 [384], replicated
- pointwise_kernel_gradient: float32 [384, 768], replicated
- pointwise_bias_gradient: float32 [768], replicated
Inputs may be any that keep to these rules, and one draw needn't show every extreme that they name: `lengths`: valid rows of a window come first; some window is full with 1024 rows and some has exactly 128. `assignment`: each row lists the 16 windows of one group once.
All inputs are finite; a program needn't handle non-finite values.
Results may differ from a plain program's by a relative error of at most 0.0066.
Values may be sent and summed in bfloat16 or wider, within the bound.
No kernel may reach another device: no remote copies, remote signals or barrier semaphores. Data moves between devices by JAX's collectives and lax.ppermute only.
A program may use at most 128 MiB of HBM per device.

v0:
```python
import jax
import jax.numpy as jnp
from jax import lax
from jax.sharding import PartitionSpec as P

DILATION_STEP = 38
WINDOW_SPAN = 1024
HALF_WINDOW_ROWS = 512
EPSILON = 0.001


def from_partner(block, axis, bit):
    count = lax.axis_size(axis)
    route = []
    for low in range(count):
        high = low | 1 << bit
        if high != low and high < count:
            route += [(low, high), (high, low)]
    return lax.ppermute(block, axis, route)


def smooth(values):
    return jax.nn.gelu(values, approximate=True)


def moments(values, valid_mask, row_count):
    centre = lax.psum(jnp.sum(values * valid_mask, axis=(0, 1)), ("grp", "seq")) / row_count
    deviation = (values - centre) * valid_mask
    spread = lax.psum(jnp.sum(deviation * deviation, axis=(0, 1)), ("grp", "seq")) / row_count
    return (centre, lax.rsqrt(spread + EPSILON))


def extended(resident_rows, neighbour_border):
    position_count = resident_rows.shape[0]
    channel_width = resident_rows.shape[2]
    empty_row_block = jnp.zeros((position_count, DILATION_STEP, channel_width), resident_rows.dtype)
    bottom_portion = jnp.concatenate(
        [empty_row_block, resident_rows[:, :HALF_WINDOW_ROWS], neighbour_border[:, DILATION_STEP:]],
        axis=1,
    )
    top_portion = jnp.concatenate(
        [neighbour_border[:, :DILATION_STEP], resident_rows[:, HALF_WINDOW_ROWS:], empty_row_block],
        axis=1,
    )
    return jnp.stack([bottom_portion, top_portion], axis=1).reshape(
        2 * position_count, HALF_WINDOW_ROWS + 2 * DILATION_STEP, channel_width
    )


def per_device(
    signal,
    entry_gain,
    entry_shift,
    dilated_kernel,
    middle_gain,
    middle_shift,
    pointwise_kernel,
    pointwise_bias,
    lengths,
    assignment,
    cotangent,
):
    seq_count = lax.axis_size("seq")
    seq_place = lax.axis_index("seq")
    grp_place = lax.axis_index("grp")
    group_windows, segment, channel_width = signal.shape
    source_rows = segment // 2
    position_count = group_windows // seq_count
    bin_pairs = signal.reshape(group_windows, source_rows, 2, channel_width)
    first_bin = bin_pairs[:, :, 0]
    second_bin = bin_pairs[:, :, 1]
    take_first = first_bin >= second_bin
    group_lengths = lax.dynamic_slice_in_dim(lengths, grp_place * group_windows, group_windows)
    source_position = seq_place * source_rows + jnp.arange(source_rows, dtype=jnp.int32)
    source_valid = (source_position[None, :] < group_lengths[:, None]).astype(jnp.float32)[
        :, :, None
    ]
    pooled_low = (jnp.where(take_first, first_bin, second_bin) * source_valid).astype(jnp.bfloat16)
    window_order = assignment[0]
    upper_source = (seq_place >= seq_count // 2).astype(jnp.int32)
    targets = jnp.arange(seq_count, dtype=jnp.int32)
    slot_range = jnp.arange(position_count, dtype=jnp.int32)
    picked = window_order[
        (
            jnp.bitwise_xor(targets, upper_source)[:, None] * position_count + slot_range[None, :]
        ).reshape(-1)
    ]
    outgoing = jnp.take(pooled_low, picked, axis=0)
    arrived = lax.all_to_all(outgoing, "seq", split_axis=0, concat_axis=1, tiled=True)
    partner_place = jnp.bitwise_xor(seq_place, 1)
    own_windows = lax.dynamic_slice_in_dim(window_order, seq_place * position_count, position_count)
    partner_windows = lax.dynamic_slice_in_dim(
        window_order, partner_place * position_count, position_count
    )
    row_position = jnp.arange(WINDOW_SPAN, dtype=jnp.int32)
    limit_rows = jnp.where(
        row_position[None, :] < HALF_WINDOW_ROWS,
        jnp.take(group_lengths, own_windows)[:, None],
        jnp.take(group_lengths, partner_windows)[:, None],
    )
    valid_mask = (row_position[None, :] < limit_rows).astype(jnp.float32)[:, :, None]
    row_count = jnp.sum(lengths.astype(jnp.float32))
    pooled = arrived.astype(jnp.float32)
    entry_centre, entry_scale = moments(pooled, valid_mask, row_count)
    entry_norm = (pooled - entry_centre) * entry_scale
    entry_smooth, entry_back = jax.vjp(smooth, entry_norm * entry_gain + entry_shift)
    entry_activation = (entry_smooth * valid_mask).astype(jnp.bfloat16)
    kernel_low = dilated_kernel.astype(jnp.bfloat16)
    entry_border = from_partner(
        entry_activation[:, HALF_WINDOW_ROWS - DILATION_STEP : HALF_WINDOW_ROWS + DILATION_STEP],
        "seq",
        0,
    )
    entry_widened = extended(entry_activation, entry_border)
    dilated_out = jnp.zeros(
        (2 * position_count, HALF_WINDOW_ROWS, kernel_low.shape[2]), jnp.float32
    )
    for kernel_tap_index in range(3):
        displaced_rows = entry_widened[
            :,
            kernel_tap_index * DILATION_STEP : kernel_tap_index * DILATION_STEP + HALF_WINDOW_ROWS,
        ]
        dilated_out = dilated_out + jnp.einsum(
            "hrc,cf->hrf",
            displaced_rows,
            kernel_low[kernel_tap_index],
            preferred_element_type=jnp.float32,
        )
    dilated_out = dilated_out.reshape(position_count, WINDOW_SPAN, -1)
    middle_centre, middle_scale = moments(dilated_out, valid_mask, row_count)
    middle_norm = (dilated_out - middle_centre) * middle_scale
    middle_smooth, middle_back = jax.vjp(smooth, middle_norm * middle_gain + middle_shift)
    middle_act = (middle_smooth * valid_mask).astype(jnp.bfloat16)
    pointwise_low = pointwise_kernel.astype(jnp.bfloat16)
    mixed_out = jnp.einsum(
        "krf,fd->krd", middle_act, pointwise_low, preferred_element_type=jnp.float32
    )
    activations = (valid_mask * (pooled + mixed_out + pointwise_bias)).reshape(-1, channel_width)
    grad_block = cotangent.reshape(position_count, WINDOW_SPAN, channel_width) * valid_mask
    grad_mixed = grad_block.astype(jnp.bfloat16)
    bias_part = jnp.sum(grad_block, axis=(0, 1))
    pointwise_part = jnp.einsum(
        "krf,krd->fd", middle_act, grad_mixed, preferred_element_type=jnp.float32
    )
    grad_middle = jnp.einsum(
        "krd,fd->krf", grad_mixed, pointwise_low, preferred_element_type=jnp.float32
    )
    grad_middle_pre = middle_back(grad_middle * valid_mask)[0]
    middle_gain_part = jnp.sum(grad_middle_pre * middle_norm, axis=(0, 1))
    middle_shift_part = jnp.sum(grad_middle_pre, axis=(0, 1))
    (
        middle_gain_gradient,
        middle_shift_gradient,
        pointwise_kernel_gradient,
        pointwise_bias_gradient,
    ) = lax.psum((middle_gain_part, middle_shift_part, pointwise_part, bias_part), ("grp", "seq"))
    dilated_gradient = (
        middle_gain
        * middle_scale
        * (
            grad_middle_pre
            - (middle_shift_gradient + middle_norm * middle_gain_gradient) / row_count
        )
        * valid_mask
    )
    dilated_gradient = dilated_gradient.astype(jnp.bfloat16)
    border_gradient = from_partner(
        dilated_gradient[:, HALF_WINDOW_ROWS - DILATION_STEP : HALF_WINDOW_ROWS + DILATION_STEP],
        "seq",
        0,
    )
    grad_wide = extended(dilated_gradient, border_gradient)
    grad_halves = dilated_gradient.reshape(2 * position_count, HALF_WINDOW_ROWS, -1)
    kernel_pieces = []
    grad_entry = jnp.zeros((2 * position_count, HALF_WINDOW_ROWS, channel_width), jnp.float32)
    for kernel_tap_index in range(3):
        displaced_rows = entry_widened[
            :,
            kernel_tap_index * DILATION_STEP : kernel_tap_index * DILATION_STEP + HALF_WINDOW_ROWS,
        ]
        kernel_pieces.append(
            jnp.einsum(
                "hrc,hrf->cf", displaced_rows, grad_halves, preferred_element_type=jnp.float32
            )
        )
        backward_offset = (2 - kernel_tap_index) * DILATION_STEP
        grad_shifted = grad_wide[:, backward_offset : backward_offset + HALF_WINDOW_ROWS]
        grad_entry = grad_entry + jnp.einsum(
            "hrf,cf->hrc",
            grad_shifted,
            kernel_low[kernel_tap_index],
            preferred_element_type=jnp.float32,
        )
    kernel_part = jnp.stack(kernel_pieces)
    grad_entry = grad_entry.reshape(position_count, WINDOW_SPAN, channel_width)
    grad_entry_pre = entry_back(grad_entry * valid_mask)[0]
    entry_gain_part = jnp.sum(grad_entry_pre * entry_norm, axis=(0, 1))
    entry_shift_part = jnp.sum(grad_entry_pre, axis=(0, 1))
    entry_gain_gradient, entry_shift_gradient, dilated_kernel_gradient = lax.psum(
        (entry_gain_part, entry_shift_part, kernel_part), ("grp", "seq")
    )
    grad_pooled = (
        entry_gain
        * entry_scale
        * (grad_entry_pre - (entry_shift_gradient + entry_norm * entry_gain_gradient) / row_count)
        * valid_mask
        + grad_block
    )
    returned = lax.all_to_all(
        grad_pooled.astype(jnp.bfloat16), "seq", split_axis=1, concat_axis=0, tiled=True
    )
    inverse = (
        jnp.zeros((group_windows,), jnp.int32)
        .at[picked]
        .set(jnp.arange(group_windows, dtype=jnp.int32))
    )
    grad_source = jnp.take(returned, inverse, axis=0).astype(jnp.float32) * source_valid
    zero_part = jnp.zeros_like(grad_source)
    signal_gradient = jnp.stack(
        [
            jnp.where(take_first, grad_source, zero_part),
            jnp.where(take_first, zero_part, grad_source),
        ],
        axis=2,
    ).reshape(group_windows, segment, channel_width)
    return (
        activations,
        signal_gradient,
        entry_gain_gradient,
        entry_shift_gradient,
        dilated_kernel_gradient,
        middle_gain_gradient,
        middle_shift_gradient,
        pointwise_kernel_gradient,
        pointwise_bias_gradient,
    )


def solution(mesh):
    return jax.shard_map(
        per_device,
        mesh=mesh,
        in_specs=(
            P("grp", "seq", None),
            P(),
            P(),
            P(),
            P(),
            P(),
            P(),
            P(),
            P(),
            P("grp", None),
            P(("grp", "seq"), None),
        ),
        out_specs=(
            P(("grp", "seq"), None),
            P("grp", "seq", None),
            P(),
            P(),
            P(),
            P(),
            P(),
            P(),
            P(),
        ),
        check_vma=False,
    )
```

profile of v0, /device:TPU:0, one launch (start us, length us, event | category | flops | bytes accessed | tf_op | source)
XLA Modules:
  0.0 660.3 jit_solution(9878125855591612174)
XLA Ops:
  8.7 16.6 %copy.79 = f32[16,256,768]{2,0,1:T(8,128)} copy(f32[16,256,768]{2,1,0:T(8,128)} %param.15) | data formatting | bytes 25165824 | tf_op args[0]
  25.4 10.5 %fusion.86 = (f32[16,128,1,768]{3,0,2,1:T(8,128)}, f32[16,128,1,768]{3,0,2,1:T(8,128)}) fusion(f32[16,128,2,768]{3,0,2,1:T(8,128)} %bitcast.168), kind=kLoop, calls=%fused_computation.166 | loop fusion | bytes 25165824 | tf_op jit(solution)/shard_map/slice | solution.py:71
  36.1 11.7 %multiply_convert_fusion.1 = (bf16[16,128,768]{2,1,0:T(8,128)(2,1)}, pred[16,128,768]{2,1,0:T(8,128)(4,1)}) fusion(f32[16,128,1,768]{3,0,2,1:T(8,128)} %get-tuple-element.66, f32[16,128,1,768]{3,0,2,1:T(8,128)} %get-tuple-element.65, f32[16,128]{1,0:T(8,128)S(1)} %compare_convert_fusion.2), kind=kLoop, calls=%fused_computation.48 | loop fusion | flops 6291456 | bytes 17309696 | tf_op jit(solution)/shard_map/convert_element_type | solution.py:78
  52.4 7.4 %all-to-all-start = ((bf16[16,128,768]{2,1,0:T(8,128)(2,1)}), bf16[16,128,768]{2,1,0:T(8,128)(2,1)S(1)}, u32[]{:S(2)}, u32[]{:S(2)}) async-start(bf16[16,128,768]{2,1,0:T(8,128)(2,1)} %broadcast_select_fusion.1), calls=%async_computation | async-start | bytes 6291456 | tf_op jit(solution)/shard_map/all_to_all | solution.py:89
  61.7 3.7 convert_element_type.105
  66.3 5.2 multiply_convert_fusion.2
  71.5 3.5 fusion.38
  75.1 55.5 %all-to-all-done = bf16[16,128,768]{2,1,0:T(8,128)(2,1)S(1)} async-done(((bf16[16,128,768]{2,1,0:T(8,128)(2,1)}), bf16[16,128,768]{2,1,0:T(8,128)(2,1)S(1)}, u32[]{:S(2)}, u32[]{:S(2)}) %all-to-all-start) | async-done | bytes 3145760 | tf_op jit(solution)/shard_map/all_to_all | solution.py:89
  131.3 37.8 %psum.77 = f32[768]{0:T(1024)S(1)} all-reduce(f32[768]{0:T(1024)S(1)} %multiply_reduce_fusion.2), channel_id=1, replica_groups=mesh['grp'=4,'seq'=8] {'grp','seq'}, use_global_device_ids=true, to_apply=%region_1.4 | all-reduce | flops 768 | bytes 6144 | tf_op jit(solution)/shard_map/psum | solution.py:27
  170.8 41.7 %psum.78 = f32[768]{0:T(1024)S(1)} all-reduce(f32[768]{0:T(1024)S(1)} %multiply_reduce_fusion.1), channel_id=1, replica_groups=mesh['grp'=4,'seq'=8] {'grp','seq'}, use_global_device_ids=true, to_apply=%region_4.7 | all-reduce | flops 768 | bytes 6144 | tf_op jit(solution)/shard_map/psum | solution.py:29
  214.6 3.4 multiply_convert_fusion
  220.6 4.9 collective-permute-done
  234.9 38.2 %psum.79 = f32[384]{0:T(512)S(1)} all-reduce(f32[384]{0:T(512)S(1)} %get-tuple-element.86), channel_id=1, replica_groups=mesh['grp'=4,'seq'=8] {'grp','seq'}, use_global_device_ids=true, to_apply=%region_6.9 | all-reduce | flops 384 | bytes 3072 | tf_op jit(solution)/shard_map/psum | solution.py:27
  274.2 41.7 %psum.80 = f32[384]{0:T(512)S(1)} all-reduce(f32[384]{0:T(512)S(1)} %multiply_reduce_fusion.5), channel_id=1, replica_groups=mesh['grp'=4,'seq'=8] {'grp','seq'}, use_global_device_ids=true, to_apply=%region_8.11 | all-reduce | flops 384 | bytes 3072 | tf_op jit(solution)/shard_map/psum | solution.py:29
  316.6 6.1 fusion.81
  322.7 38.7 %all-reduce.1 = (f32[384]{0:T(512)S(1)}, f32[384]{0:T(512)S(1)}) all-reduce(f32[384]{0:T(512)S(1)} %get-tuple-element.50, f32[384]{0:T(512)S(1)} %get-tuple-element.49), channel_id=1, replica_groups=mesh['grp'=4,'seq'=8] {'grp','seq'}, use_global_device_ids=true, to_apply=%region_12.15 | all-reduce | flops 768 | bytes 6144 | tf_op jit(solution)/shard_map/psum | solution.py:156
  361.4 3.0 multiply_convert_fusion.5
  367.0 2.7 collective-permute-done.1
  375.3 8.2 %fusion.80 = (f32[768]{0:T(1024)S(1)}, f32[768]{0:T(1024)S(1)}, f32[4,512,768]{2,1,0:T(8,128)}) fusion(f32[768]{0:T(1024)S(1)} %get-tuple-element.59, f32[4,512,768]{2,1,0:T(8,128)S(1)} %bitcast.163, f32[768]{0:T(1024)S(1)} %broadcast_divide_fusion, f32[768]{0:T(1024)S(1)} %copy-done.15, f32[768]{0:T(1024)S(1)} %copy-done.13, f32[4,512]{1,0:T(4,128)S(1)} %fusion.74, ...), kind=kOutput, calls=%fused_computation.162 | convolution fusion | flops 1253571072 | bytes 27359232 | tf_op jit(solution)/shard_map/hrf,cf->hrc/dot_general | solution.py:188
  383.5 41.3 %all-reduce = (f32[768]{0:T(1024)S(1)}, f32[768]{0:T(1024)S(1)}, f32[768]{0:T(1024)}) all-reduce(f32[768]{0:T(1024)S(1)} %get-tuple-element.48, f32[768]{0:T(1024)S(1)} %get-tuple-element.47, f32[768]{0:T(1024)S(1)} %get-tuple-element.68), channel_id=1, replica_groups=mesh['grp'=4,'seq'=8] {'grp','seq'}, use_global_device_ids=true, to_apply=%region_16.19 | all-reduce | flops 2304 | bytes 18432 | tf_op jit(solution)/shard_map/psum | solution.py:199
  424.8 11.1 %fusion.10 = bf16[2,1024,768]{2,1,0:T(8,128)(2,1)S(1)} fusion(f32[2,1024,768]{2,1,0:T(8,128)} %bitcast.164, f32[2,8,128,768]{3,2,1,0:T(8,128)} %copy-done.1, f32[]{:T(128)} %convert_reduce_fusion, f32[768]{0:T(1024)S(1)} %get-tuple-element.95, f32[768]{0:T(1024)S(1)} %get-tuple-element.96, f32[768]{0:T(1024)S(1)} %get-tuple-element.58, ...), kind=kLoop, calls=%fused_computation.21 | loop fusion | flops 51904512 | bytes 22049796 | tf_op jit(solution)/shard_map/convert_element_type | solution.py:210
  435.9 5.0 copy.86
  440.9 5.2 all-to-all-start.1
  446.2 4.3 fusion.60
  462.3 7.3 %fusion.19 = f32[2,1024,768]{2,1,0:T(8,128)} fusion(f32[2,8,128,768]{3,2,1,0:T(8,128)} %copy-done.1, f32[768]{0:T(1024)S(1)} %copy-done.17, f32[2,1024]{1,0:T(2,128)S(1)} %compare_convert_fusion.1, bf16[2,1024,384]{2,1,0:T(8,128)(2,1)S(1)} %copy-done.5, f32[384,768]{1,0:T(8,128)S(1)} %copy-done.7), kind=kOutput, calls=%fused_computation.36 | convolution fusion | flops 1212973056 | bytes 15346688 | tf_op jit(solution)/shard_map/krf,fd->krd/dot_general | solution.py:135
  469.6 68.6 %all-to-all-done.1 = bf16[2,1024,768]{2,0,1:T(2,128)(2,1)} async-done(((bf16[2,1024,768]{2,0,1:T(2,128)(2,1)}), bf16[2,1024,768]{2,0,1:T(2,128)(2,1)}, u32[]{:S(2)}, u32[]{:S(2)}) %all-to-all-start.1) | async-done | bytes 3145760 | tf_op jit(solution)/shard_map/all_to_all | solution.py:209
  543.1 5.3 select_bitcast_fusion.1
  548.4 9.2 %pad_maximum_fusion = f32[16,128,2,768]{3,1,0,2:T(8,128)} fusion(f32[16,128,1,768]{3,1,0,2:T(8,128)} %get-tuple-element.70, f32[16,128,1,768]{3,1,0,2:T(8,128)S(1)} %get-tuple-element.69), kind=kLoop, calls=%fused_computation.6 | loop fusion | flops 3145728 | bytes 25165824 | tf_op jit(solution)/shard_map/stack | solution.py:219
  557.6 16.5 %copy.89 = f32[16,128,2,768]{3,0,2,1:T(8,128)} copy(f32[16,128,2,768]{3,1,0,2:T(8,128)} %pad_maximum_fusion) | data formatting | bytes 25165824 | tf_op jit(solution)/shard_map/stack | solution.py:219
  574.0 16.9 %copy.94 = f32[16,256,768]{2,1,0:T(8,128)} copy(f32[16,256,768]{2,0,1:T(8,128)} %bitcast.169) | data formatting | bytes 25165824
  590.9 57.0 %all-reduce.5.cloned.1.call-done = (f32[3,768,384]{2,1,0:T(8,128)}, f32[384,768]{1,0:T(8,128)}) async-done(((f32[3,768,384]{2,1,0:T(8,128)}, f32[384,768]{1,0:T(8,128)}), (f32[3,768,384]{2,1,0:T(8,128)}, f32[384,768]{1,0:T(8,128)})) %all-reduce.5.cloned.1.call-update) | async-done | bytes 4718608 | tf_op jit(solution)/shard_map/psum | solution.py:199
  647.9 4.1 copy.127
  (144 shorter events, 53.0 us)
Async XLA Ops:
  25.4 10.5 %copy-start.22 = (s32[64]{0:T(128)S(1)}, s32[64]{0:T(128)}, u32[]{:S(2)}) copy-start(s32[64]{0:T(128)} %param.23) | copy-start | bytes 772
  52.4 7.5 %copy-start = (s32[1,16]{1,0:T(1,128)S(1)}, s32[1,16]{1,0:T(1,128)}, u32[]{:S(2)}) copy-start(s32[1,16]{1,0:T(1,128)} %param.24) | copy-start | bytes 196
  52.4 78.1 %all-to-all-start = ((bf16[16,128,768]{2,1,0:T(8,128)(2,1)}), bf16[16,128,768]{2,1,0:T(8,128)(2,1)S(1)}, u32[]{:S(2)}, u32[]{:S(2)}) async-start(bf16[16,128,768]{2,1,0:T(8,128)(2,1)} %broadcast_select_fusion.1), calls=%async_computation | async-start | bytes 6291456 | tf_op jit(solution)/shard_map/all_to_all | solution.py:89
  61.7 9.9 %slice-start.2 = ((s8[6291456]{0:T(1024)(128)(4,1)}), s8[4194304]{0:T(1024)(128)(4,1)S(1)}, s32[]{:S(2)}) async-start(s8[6291456]{0:T(1024)(128)(4,1)} %bitcast.165), calls=%async_computation.5 | async-start | bytes 8388608
  66.3 5.2 slice-start.3
  66.3 5.2 copy-start.6
  213.2 0.7 copy-start.13
  213.2 1.3 copy-start.15
  213.9 4.1 copy-start.1
  218.1 7.4 %collective-permute-start = (bf16[2,76,768]{2,1,0:T(8,128)(2,1)S(1)}, bf16[2,76,768]{2,1,0:T(8,128)(2,1)S(1)}, u32[]{:S(2)}, u32[]{:S(2)}) collective-permute-start(bf16[2,76,768]{2,1,0:T(8,128)(2,1)S(1)} %slice.103), channel_id=1, source_target_pairs={{0,1},{1,0},{2,3},{3,2},{4,5},{5,4},{6,7},{7,6},{8,9},{9,8},{10,11... | collective-permute-start | bytes 700424 | tf_op jit(solution)/shard_map/ppermute | solution.py:19
  227.0 2.1 copy-start.10
  227.3 5.6 copy-start.8
  234.9 81.1 %copy-start.14 = (f32[384]{0:T(512)S(1)}, f32[384]{0:T(512)}, u32[]{:S(2)}) copy-start(f32[384]{0:T(512)} %param.19) | copy-start | bytes 4612
  234.9 81.7 %copy-start.16 = (f32[384]{0:T(512)S(1)}, f32[384]{0:T(512)}, u32[]{:S(2)}) copy-start(f32[384]{0:T(512)} %param.20) | copy-start | bytes 4612
  361.4 3.1 copy-start.20
  361.4 3.1 copy-start.21
  364.4 2.4 copy-start.3
  364.5 5.2 collective-permute-start.1
  370.2 1.5 copy-start.11
  370.4 4.9 slice-start
  371.6 3.7 slice-start.1
  424.8 11.1 %copy-start.18 = (f32[768]{0:T(1024)}, f32[768]{0:T(1024)S(1)}, u32[]{:S(2)}) copy-start(f32[768]{0:T(1024)S(1)} %get-tuple-element.95) | copy-start | bytes 9220
  424.8 11.1 %copy-start.19 = (f32[768]{0:T(1024)}, f32[768]{0:T(1024)S(1)}, u32[]{:S(2)}) copy-start(f32[768]{0:T(1024)S(1)} %get-tuple-element.96) | copy-start | bytes 9220
  440.9 97.2 %all-to-all-start.1 = ((bf16[2,1024,768]{2,0,1:T(2,128)(2,1)}), bf16[2,1024,768]{2,0,1:T(2,128)(2,1)}, u32[]{:S(2)}, u32[]{:S(2)}) async-start(bf16[2,1024,768]{2,0,1:T(2,128)(2,1)} %copy.86), calls=%async_computation.1 | async-start | bytes 6291456 | tf_op jit(solution)/shard_map/all_to_all | solution.py:209
  446.1 201.8 %all-reduce.5.cloned.1.call-start = ((), (), s32[]{:S(2)}) async-start(), calls=%async_computation.2 | async-start | bytes 9437184 | tf_op jit(solution)/shard_map/psum | solution.py:199
  446.2 4.3 copy-start.4
  446.2 4.3 copy-start.9
  456.2 1.9 copy-start.2
  460.5 1.4 copy-start.5
  460.5 1.7 copy-start.7
  460.5 1.7 copy-start.17
  647.9 4.1 copy-start.12
Sparse Core Ops, SparseCore 0:
  460.7 187.1 all-reduce.4
where the time goes:
time: 668 us; the launch traced here: 660 us
  blocking collectives  239 us (36%)
  waiting for transfers between devices  189 us (28%)
  local copies, waits for them, and re-layouts  88.1 us (13%)
  other arithmetic  73 us (11%)
  matrix products  38.7 us (6%)
  starting transfers between devices  17.3 us (3%)
  between operations  15.1 us (2%)
    psum x2, blocking collectives, moments(): lax.psum(jnp.sum(deviation * deviation, axis=(0, 1)), ('grp', 'seq'))  83.4 us
    psum x2, blocking collectives, moments(): lax.psum(jnp.sum(values * valid_mask, axis=(0, 1)), ('grp', 'seq'))  76 us
    all_to_all x1, waiting for transfers between devices, per_device(): lax.all_to_all(grad_pooled.astype(jnp.bfloat16), 'seq', split_axis=1, con...  68.6 us
    psum x1, waiting for transfers between devices, per_device(): lax.psum((entry_gain_part, entry_shift_part, kernel_part), ('grp', 'seq'))  57 us
    all_to_all x1, waiting for transfers between devices, per_device(): lax.all_to_all(outgoing, 'seq', split_axis=0, concat_axis=1, tiled=True)  55.5 us
    unnamed x61, local copies, waits for them, and re-layouts  43.3 us
    psum x1, blocking collectives, per_device(): lax.psum((entry_gain_part, entry_shift_part, kernel_part), ('grp', 'seq'))  41.3 us
    psum x1, blocking collectives, per_device(): lax.psum((middle_gain_part, middle_shift_part, pointwise_part, bias_part)...  38.7 us
  transfers between devices with their start and end apart: 5, of which 5 were waited for; matrix products, arithmetic and copies ran while one was open for 14% of the time, Pallas kernels for 0%

commit v1 on v0

--- a/solution.py
+++ b/solution.py
@@ -7,6 +7,28 @@
 WINDOW_SPAN = 1024
 HALF_WINDOW_ROWS = 512
 EPSILON = 0.001
+
+
+def in_blocks(shard, dim, devices):
+    before, after = (shard.shape[:dim], shard.shape[dim + 1 :])
+    return jnp.moveaxis(shard.reshape(*before, devices, -1, *after), dim, 0)
+
+
+def laid_out(pieces, dim):
+    pieces = jnp.moveaxis(pieces, 0, dim)
+    shape = pieces.shape
+    return pieces.reshape(*shape[:dim], shape[dim] * shape[dim + 1], *shape[dim + 2 :])
+
+
+def pairwise_exchange(value, axis, split_dim, concat_dim):
+    peers, index = (lax.axis_size(axis), lax.axis_index(axis))
+    parts = in_blocks(value, split_dim, peers)
+    outs = [parts[index]]
+    for step in range(1, peers):
+        sent = parts[index ^ step]
+        outs.append(lax.ppermute(sent, axis, [(i, i ^ step) for i in range(peers)]))
+    parts = jnp.stack(outs)[index ^ jnp.arange(peers)]
+    return laid_out(parts, concat_dim)
 
 
 def from_partner(block, axis, bit):
@@ -86,7 +108,7 @@
         ).reshape(-1)
     ]
     outgoing = jnp.take(pooled_low, picked, axis=0)
-    arrived = lax.all_to_all(outgoing, "seq", split_axis=0, concat_axis=1, tiled=True)
+    arrived = pairwise_exchange(outgoing, "seq", 0, 1)
     partner_place = jnp.bitwise_xor(seq_place, 1)
     own_windows = lax.dynamic_slice_in_dim(window_order, seq_place * position_count, position_count)
     partner_windows = lax.dynamic_slice_in_dim(

time: 668 us -> 678 us (1.015)
  local copies, waits for them, and re-layouts: 88.1 us -> 105 us
  waiting for transfers between devices: 189 us -> 173 us
    all_to_all x1 -> x0, waiting for transfers between devices: 55.5 us -> none  [per_device(): lax.all_to_all(outgoing, 'seq', split_axis=0, concat_axis=1, tiled=True)]
    ppermute x0 -> x7, waiting for transfers between devices: none -> 41.2 us  [pairwise_exchange(): outs.append(lax.ppermute(sent, axis, [(i, i ^ step) for i in range(peers)]))]
    ppermute x0 -> x7, starting transfers between devices: none -> 13.1 us  [pairwise_exchange(): outs.append(lax.ppermute(sent, axis, [(i, i ^ step) for i in range(peers)]))]
    all_to_all x1 -> x0, starting transfers between devices: 7.41 us -> none  [per_device(): lax.all_to_all(outgoing, 'seq', split_axis=0, concat_axis=1, tiled=True)]
    unnamed x61 -> x85, local copies, waits for them, and re-layouts: 43.3 us -> 50.4 us
  transfers between devices with their start and end apart: 5 -> 11, of which waited for: 5 -> 7; matrix products, arithmetic and copies ran while one was open for 14% -> 14% of each run, Pallas kernels for 0% -> 0%
where the time goes in v1:
time: 678 us; the launch traced here: 670 us
  blocking collectives  240 us (35%)
  waiting for transfers between devices  173 us (26%)
  local copies, waits for them, and re-layouts  105 us (15%)
  other arithmetic  75.4 us (11%)
  matrix products  38.7 us (6%)
  starting transfers between devices  23.5 us (3%)
  between operations  15.2 us (2%)
    psum x2, blocking collectives, moments(): lax.psum(jnp.sum(deviation * deviation, axis=(0, 1)), ('grp', 'seq'))  83.2 us
    psum x2, blocking collectives, moments(): lax.psum(jnp.sum(values * valid_mask, axis=(0, 1)), ('grp', 'seq'))  76.3 us
    all_to_all x1, waiting for transfers between devices, per_device(): lax.all_to_all(grad_pooled.astype(jnp.bfloat16), 'seq', split_axis=1, con...  68.5 us
    psum x1, waiting for transfers between devices, per_device(): lax.psum((entry_gain_part, entry_shift_part, kernel_part), ('grp', 'seq'))  56.2 us
    unnamed x85, local copies, waits for them, and re-layouts  50.4 us
    ppermute x7, waiting for transfers between devices, pairwise_exchange(): outs.append(lax.ppermute(sent, axis, [(i, i ^ step) for i in range(peers)]))  41.2 us
    psum x1, blocking collectives, per_device(): lax.psum((entry_gain_part, entry_shift_part, kernel_part), ('grp', 'seq'))  40.9 us
    psum x1, blocking collectives, per_device(): lax.psum((middle_gain_part, middle_shift_part, pointwise_part, bias_part)...  39.1 us
  transfers between devices with their start and end apart: 11, of which 7 were waited for; matrix products, arithmetic and copies ran while one was open for 14% of the time, Pallas kernels for 0%

profile of v1, /device:TPU:0, one launch (start us, length us, event | category | flops | bytes accessed | tf_op | source)
XLA Modules:
  0.0 670.4 jit_solution(6710531502237355332)
XLA Ops:
  9.3 16.6 %copy.79 = f32[16,256,768]{2,0,1:T(8,128)} copy(f32[16,256,768]{2,1,0:T(8,128)} %param.15) | data formatting | bytes 25165824 | tf_op args[0]
  25.9 10.5 %fusion.89 = (f32[16,128,1,768]{3,0,2,1:T(8,128)}, f32[16,128,1,768]{3,0,2,1:T(8,128)}) fusion(f32[16,128,2,768]{3,0,2,1:T(8,128)} %bitcast.200), kind=kLoop, calls=%fused_computation.189 | loop fusion | bytes 25165824 | tf_op jit(solution)/shard_map/slice | solution.py:93
  36.6 11.4 %multiply_convert_fusion.1 = (bf16[16,128,768]{2,1,0:T(8,128)(2,1)}, pred[16,128,768]{2,1,0:T(8,128)(4,1)}) fusion(f32[16,128,1,768]{3,0,2,1:T(8,128)} %get-tuple-element.66, f32[16,128,1,768]{3,0,2,1:T(8,128)} %get-tuple-element.65, f32[16,128]{1,0:T(8,128)S(1)} %compare_convert_fusion.2), kind=kLoop, calls=%fused_computation.49 | loop fusion | flops 6291456 | bytes 17309696 | tf_op jit(solution)/shard_map/convert_element_type | solution.py:100
  48.0 4.3 gather_fusion.4
  56.3 6.0 collective-permute-start.6
  70.9 5.8 multiply_convert_fusion.2
  76.7 3.5 fusion.38
  84.7 12.7 %collective-permute-done.1 = bf16[2,128,768]{2,1,0:T(8,128)(2,1)} collective-permute-done((bf16[2,128,768]{2,1,0:T(8,128)(2,1)}, bf16[2,128,768]{2,1,0:T(8,128)(2,1)}, u32[]{:S(2)}, u32[]{:S(2)}) %collective-permute-start.1) | collective-permute-done | bytes 393248 | tf_op jit(solution)/shard_map/ppermute | solution.py:29
  100.5 5.3 collective-permute-done.2
  106.6 23.2 %collective-permute-done.3 = bf16[2,128,768]{2,1,0:T(8,128)(2,1)S(1)} collective-permute-done((bf16[2,128,768]{2,1,0:T(8,128)(2,1)S(1)}, bf16[2,128,768]{2,1,0:T(8,128)(2,1)S(1)}, u32[]{:S(2)}, u32[]{:S(2)}) %collective-permute-start.3) | collective-permute-done | bytes 393248 | tf_op jit(solution)/shard_map/ppermute | solution.py:29
  139.7 37.8 %psum.77 = f32[768]{0:T(1024)S(1)} all-reduce(f32[768]{0:T(1024)S(1)} %multiply_reduce_fusion.2), channel_id=1, replica_groups=mesh['grp'=4,'seq'=8] {'grp','seq'}, use_global_device_ids=true, to_apply=%region_1.4 | all-reduce | flops 768 | bytes 6144 | tf_op jit(solution)/shard_map/psum | solution.py:49
  179.3 41.9 %psum.78 = f32[768]{0:T(1024)S(1)} all-reduce(f32[768]{0:T(1024)S(1)} %multiply_reduce_fusion.1), channel_id=1, replica_groups=mesh['grp'=4,'seq'=8] {'grp','seq'}, use_global_device_ids=true, to_apply=%region_4.7 | all-reduce | flops 768 | bytes 6144 | tf_op jit(solution)/shard_map/psum | solution.py:51
  221.2 3.5 copy.82
  231.5 4.4 collective-permute-done.7
  245.3 38.5 %psum.79 = f32[384]{0:T(512)S(1)} all-reduce(f32[384]{0:T(512)S(1)} %get-tuple-element.94), channel_id=1, replica_groups=mesh['grp'=4,'seq'=8] {'grp','seq'}, use_global_device_ids=true, to_apply=%region_6.9 | all-reduce | flops 384 | bytes 3072 | tf_op jit(solution)/shard_map/psum | solution.py:49
  284.9 41.3 %psum.80 = f32[384]{0:T(512)S(1)} all-reduce(f32[384]{0:T(512)S(1)} %multiply_reduce_fusion.5), channel_id=1, replica_groups=mesh['grp'=4,'seq'=8] {'grp','seq'}, use_global_device_ids=true, to_apply=%region_8.11 | all-reduce | flops 384 | bytes 3072 | tf_op jit(solution)/shard_map/psum | solution.py:51
  327.0 6.1 fusion.84
  333.0 39.1 %all-reduce.1 = (f32[384]{0:T(512)S(1)}, f32[384]{0:T(512)S(1)}) all-reduce(f32[384]{0:T(512)S(1)} %get-tuple-element.50, f32[384]{0:T(512)S(1)} %get-tuple-element.49), channel_id=1, replica_groups=mesh['grp'=4,'seq'=8] {'grp','seq'}, use_global_device_ids=true, to_apply=%region_12.15 | all-reduce | flops 768 | bytes 6144 | tf_op jit(solution)/shard_map/psum | solution.py:178
  386.2 8.2 %fusion.83 = (f32[768]{0:T(1024)S(1)}, f32[768]{0:T(1024)S(1)}, f32[4,512,768]{2,1,0:T(8,128)}) fusion(f32[768]{0:T(1024)S(1)} %get-tuple-element.59, f32[4,512,768]{2,1,0:T(8,128)S(1)} %bitcast.195, f32[768]{0:T(1024)S(1)} %broadcast_divide_fusion, f32[768]{0:T(1024)S(1)} %copy-done.22, f32[768]{0:T(1024)S(1)} %copy-done.19, f32[4,512]{1,0:T(4,128)S(1)} %copy-done.18, ...), kind=kOutput, calls=%fused_computation.185 | convolution fusion | flops 1253571072 | bytes 27359232 | tf_op jit(solution)/shard_map/hrf,cf->hrc/dot_general | solution.py:210
  394.3 40.9 %all-reduce = (f32[768]{0:T(1024)S(1)}, f32[768]{0:T(1024)S(1)}, f32[768]{0:T(1024)}) all-reduce(f32[768]{0:T(1024)S(1)} %get-tuple-element.48, f32[768]{0:T(1024)S(1)} %get-tuple-element.47, f32[768]{0:T(1024)S(1)} %copy-done.21), channel_id=1, replica_groups=mesh['grp'=4,'seq'=8] {'grp','seq'}, use_global_device_ids=true, to_apply=%region_16.19 | all-reduce | flops 2304 | bytes 18432 | tf_op jit(solution)/shard_map/psum | solution.py:221
  435.2 11.1 %fusion.10 = bf16[2,1024,768]{2,1,0:T(8,128)(2,1)S(1)} fusion(f32[2,1024,768]{2,1,0:T(8,128)} %bitcast.196, f32[2,8,128,768]{3,2,1,0:T(8,128)} %copy-done.1, f32[]{:T(128)} %convert_reduce_fusion, f32[768]{0:T(1024)S(1)} %get-tuple-element.103, f32[768]{0:T(1024)S(1)} %get-tuple-element.104, f32[768]{0:T(1024)S(1)} %get-tuple-element.58, ...), kind=kLoop, calls=%fused_computation.22 | loop fusion | flops 51904512 | bytes 22049796 | tf_op jit(solution)/shard_map/convert_element_type | solution.py:232
  446.4 4.9 copy.86
  451.3 5.7 all-to-all-start
  457.0 4.3 fusion.60
  473.1 7.3 %fusion.19 = f32[2,1024,768]{2,1,0:T(8,128)} fusion(f32[2,8,128,768]{3,2,1,0:T(8,128)} %copy-done.1, f32[768]{0:T(1024)S(1)} %copy-done.24, f32[2,1024]{1,0:T(2,128)S(1)} %compare_convert_fusion.1, bf16[2,1024,384]{2,1,0:T(8,128)(2,1)S(1)} %copy-done.5, f32[384,768]{1,0:T(8,128)S(1)} %copy-done.7), kind=kOutput, calls=%fused_computation.36 | convolution fusion | flops 1212973056 | bytes 15346688 | tf_op jit(solution)/shard_map/krf,fd->krd/dot_general | solution.py:157
  480.5 68.5 %all-to-all-done = bf16[2,1024,768]{2,0,1:T(2,128)(2,1)} async-done(((bf16[2,1024,768]{2,0,1:T(2,128)(2,1)}), bf16[2,1024,768]{2,0,1:T(2,128)(2,1)}, u32[]{:S(2)}, u32[]{:S(2)}) %all-to-all-start) | async-done | bytes 3145760 | tf_op jit(solution)/shard_map/all_to_all | solution.py:231
  553.9 5.3 select_bitcast_fusion.1
  559.1 9.1 %pad_maximum_fusion = f32[16,128,2,768]{3,1,0,2:T(8,128)} fusion(f32[16,128,1,768]{3,1,0,2:T(8,128)} %get-tuple-element.70, f32[16,128,1,768]{3,1,0,2:T(8,128)S(1)} %get-tuple-element.69), kind=kLoop, calls=%fused_computation.7 | loop fusion | flops 3145728 | bytes 25165824 | tf_op jit(solution)/shard_map/stack | solution.py:241
  568.3 16.5 %copy.89 = f32[16,128,2,768]{3,0,2,1:T(8,128)} copy(f32[16,128,2,768]{3,1,0,2:T(8,128)} %pad_maximum_fusion) | data formatting | bytes 25165824 | tf_op jit(solution)/shard_map/stack | solution.py:241
  584.8 16.9 %copy.94 = f32[16,256,768]{2,1,0:T(8,128)} copy(f32[16,256,768]{2,0,1:T(8,128)} %bitcast.201) | data formatting | bytes 25165824
  601.7 56.2 %all-reduce.5.cloned.1.call-done = (f32[3,768,384]{2,1,0:T(8,128)}, f32[384,768]{1,0:T(8,128)}) async-done(((f32[3,768,384]{2,1,0:T(8,128)}, f32[384,768]{1,0:T(8,128)}), (f32[3,768,384]{2,1,0:T(8,128)}, f32[384,768]{1,0:T(8,128)})) %all-reduce.5.cloned.1.call-update) | async-done | bytes 4718608 | tf_op jit(solution)/shard_map/psum | solution.py:221
  657.9 4.1 copy.134
  (185 shorter events, 84.2 us)
Async XLA Ops:
  25.9 10.6 %copy-start.31 = (s32[64]{0:T(128)S(1)}, s32[64]{0:T(128)}, u32[]{:S(2)}) copy-start(s32[64]{0:T(128)} %param.23) | copy-start | bytes 772
  36.6 11.4 %copy-start.16 = (f32[16,128]{1,0:T(8,128)}, f32[16,128]{1,0:T(8,128)S(1)}, u32[]{:S(2)}) copy-start(f32[16,128]{1,0:T(8,128)S(1)} %compare_convert_fusion.2) | copy-start | bytes 24580
  54.6 14.3 %copy-start = (s32[1,16]{1,0:T(1,128)S(1)}, s32[1,16]{1,0:T(1,128)}, u32[]{:S(2)}) copy-start(s32[1,16]{1,0:T(1,128)} %param.24) | copy-start | bytes 196
  54.6 22.1 %slice-start.2 = ((s8[6291456]{0:T(1024)(128)(4,1)}), s8[2097152]{0:T(1024)(128)(4,1)S(1)}, s32[]{:S(2)}) async-start(s8[6291456]{0:T(1024)(128)(4,1)} %bitcast.197), calls=%async_computation.4 | async-start | bytes 4194304
  56.3 75.8 %collective-permute-start.6 = (bf16[2,128,768]{2,1,0:T(8,128)(2,1)}, bf16[2,128,768]{2,1,0:T(8,128)(2,1)S(1)}, u32[]{:S(2)}, u32[]{:S(2)}) collective-permute-start(bf16[2,128,768]{2,1,0:T(8,128)(2,1)} %get-tuple-element.74), channel_id=1, source_target_pairs={{0,7},{1,6},{2,5},{3,4},{4,3},{5,2},{6,1},{7,0},{8,15},{9,14},{10,... | collective-permute-start | bytes 1179656 | tf_op jit(solution)/shard_map/ppermute | solution.py:29
  62.3 69.0 %collective-permute-start.5 = (bf16[2,128,768]{2,1,0:T(8,128)(2,1)}, bf16[2,128,768]{2,1,0:T(8,128)(2,1)S(1)}, u32[]{:S(2)}, u32[]{:S(2)}) collective-permute-start(bf16[2,128,768]{2,1,0:T(8,128)(2,1)} %get-tuple-element.75), channel_id=1, source_target_pairs={{0,6},{1,7},{2,4},{3,5},{4,2},{5,3},{6,0},{7,1},{8,14},{9,15},{10,... | collective-permute-start | bytes 1179656 | tf_op jit(solution)/shard_map/ppermute | solution.py:29
  62.5 68.0 %collective-permute-start.4 = (bf16[2,128,768]{2,1,0:T(8,128)(2,1)}, bf16[2,128,768]{2,1,0:T(8,128)(2,1)S(1)}, u32[]{:S(2)}, u32[]{:S(2)}) collective-permute-start(bf16[2,128,768]{2,1,0:T(8,128)(2,1)} %get-tuple-element.76), channel_id=1, source_target_pairs={{0,5},{1,4},{2,7},{3,6},{4,1},{5,0},{6,3},{7,2},{8,13},{9,12},{10,... | collective-permute-start | bytes 1179656 | tf_op jit(solution)/shard_map/ppermute | solution.py:29
  63.3 34.2 %collective-permute-start.1 = (bf16[2,128,768]{2,1,0:T(8,128)(2,1)}, bf16[2,128,768]{2,1,0:T(8,128)(2,1)}, u32[]{:S(2)}, u32[]{:S(2)}) collective-permute-start(bf16[2,128,768]{2,1,0:T(8,128)(2,1)} %get-tuple-element.79), channel_id=1, source_target_pairs={{0,2},{1,3},{2,0},{3,1},{4,6},{5,7},{6,4},{7,5},{8,10},{9,11},{10,... | collective-permute-start | bytes 1179656 | tf_op jit(solution)/shard_map/ppermute | solution.py:29
  66.6 16.3 %collective-permute-start = (bf16[2,128,768]{2,1,0:T(8,128)(2,1)}, bf16[2,128,768]{2,1,0:T(8,128)(2,1)}, u32[]{:S(2)}, u32[]{:S(2)}) collective-permute-start(bf16[2,128,768]{2,1,0:T(8,128)(2,1)} %get-tuple-element.80), channel_id=1, source_target_pairs={{0,1},{1,0},{2,3},{3,2},{4,5},{5,4},{6,7},{7,6},{8,9},{9,8},{10,11... | collective-permute-start | bytes 1179656 | tf_op jit(solution)/shard_map/ppermute | solution.py:29
  70.9 5.8 slice-start.3
  70.9 5.8 copy-start.6
  76.7 4.3 copy-start.10
  80.2 17.3 %copy-start.14 = (bf16[2,128,768]{2,1,0:T(8,128)(2,1)S(1)}, bf16[2,128,768]{2,1,0:T(8,128)(2,1)}, u32[]{:S(2)}) copy-start(bf16[2,128,768]{2,1,0:T(8,128)(2,1)} %get-tuple-element.77) | copy-start | bytes 1179652
  83.0 22.8 %collective-permute-start.2 = (bf16[2,128,768]{2,1,0:T(8,128)(2,1)S(1)}, bf16[2,128,768]{2,1,0:T(8,128)(2,1)S(1)}, u32[]{:S(2)}, u32[]{:S(2)}) collective-permute-start(bf16[2,128,768]{2,1,0:T(8,128)(2,1)S(1)} %copy-done.15), channel_id=1, source_target_pairs={{0,3},{1,2},{2,1},{3,0},{4,7},{5,6},{6,5},{7,4},{8,11},{9,10},{10,... | collective-permute-start | bytes 1179656 | tf_op jit(solution)/shard_map/ppermute | solution.py:29
  97.5 32.3 %collective-permute-start.3 = (bf16[2,128,768]{2,1,0:T(8,128)(2,1)S(1)}, bf16[2,128,768]{2,1,0:T(8,128)(2,1)S(1)}, u32[]{:S(2)}, u32[]{:S(2)}) collective-permute-start(bf16[2,128,768]{2,1,0:T(8,128)(2,1)S(1)} %copy-done.14), channel_id=1, source_target_pairs={{0,4},{1,5},{2,6},{3,7},{4,0},{5,1},{6,2},{7,3},{8,12},{9,13},{10,... | collective-permute-start | bytes 1179656 | tf_op jit(solution)/shard_map/ppermute | solution.py:29
  221.2 4.2 copy-start.22
  224.7 4.2 copy-start.1
  228.9 6.9 %collective-permute-start.7 = (bf16[2,76,768]{2,1,0:T(8,128)(2,1)S(1)}, bf16[2,76,768]{2,1,0:T(8,128)(2,1)S(1)}, u32[]{:S(2)}, u32[]{:S(2)}) collective-permute-start(bf16[2,76,768]{2,1,0:T(8,128)(2,1)S(1)} %slice.105), channel_id=1, source_target_pairs={{0,1},{1,0},{2,3},{3,2},{4,5},{5,4},{6,7},{7,6},{8,9},{9,8},{10,11... | collective-permute-start | bytes 700424 | tf_op jit(solution)/shard_map/ppermute | solution.py:41
  237.7 5.6 copy-start.8
  245.3 81.0 %copy-start.20 = (f32[384]{0:T(512)S(1)}, f32[384]{0:T(512)}, u32[]{:S(2)}) copy-start(f32[384]{0:T(512)} %param.19) | copy-start | bytes 4612
  245.3 81.7 %copy-start.23 = (f32[384]{0:T(512)S(1)}, f32[384]{0:T(512)}, u32[]{:S(2)}) copy-start(f32[384]{0:T(512)} %param.20) | copy-start | bytes 4612
  375.3 5.2 collective-permute-start.8
  381.2 4.9 slice-start
  382.5 3.7 slice-start.1
  386.2 8.2 %copy-start.21 = (f32[768]{0:T(1024)S(1)}, f32[768]{0:T(1024)}, u32[]{:S(2)}) copy-start(f32[768]{0:T(1024)} %get-tuple-element.68) | copy-start | bytes 9220
  435.2 11.1 %copy-start.25 = (f32[768]{0:T(1024)}, f32[768]{0:T(1024)S(1)}, u32[]{:S(2)}) copy-start(f32[768]{0:T(1024)S(1)} %get-tuple-element.103) | copy-start | bytes 9220
  435.2 11.1 %copy-start.26 = (f32[768]{0:T(1024)}, f32[768]{0:T(1024)S(1)}, u32[]{:S(2)}) copy-start(f32[768]{0:T(1024)S(1)} %get-tuple-element.104) | copy-start | bytes 9220
  451.3 97.6 %all-to-all-start = ((bf16[2,1024,768]{2,0,1:T(2,128)(2,1)}), bf16[2,1024,768]{2,0,1:T(2,128)(2,1)}, u32[]{:S(2)}, u32[]{:S(2)}) async-start(bf16[2,1024,768]{2,0,1:T(2,128)(2,1)} %copy.86), calls=%async_computation | async-start | bytes 6291456 | tf_op jit(solution)/shard_map/all_to_all | solution.py:231
  457.0 200.9 %all-reduce.5.cloned.1.call-start = ((), (), s32[]{:S(2)}) async-start(), calls=%async_computation.1 | async-start | bytes 9437184 | tf_op jit(solution)/shard_map/psum | solution.py:221
  457.0 4.3 copy-start.4
  457.0 4.3 copy-start.9
  657.9 4.1 copy-start.13
  (15 other events, 30.8 us)
Sparse Core Ops, SparseCore 0:
  471.5 186.3 all-reduce.4
